TPU v7x, 32 devices: a whole 2x2x4 slice. The times are simulated.
32 devices in a mesh: rep: 2 (over y), grp: 8 (over z, x), sub: 2 (over core).
Axes of the slice: x: 2, y: 2, z: 4, core: 2. Of those that a mesh axis runs over, the one named last changes fastest.
Arguments:
- query_rows: bfloat16 [16, 4, 5120], P(('grp', 'sub'), 'rep'), parts along dimension 1, may hold values from -120 to 120
- cache_keys: bfloat16 [16, 4, 128, 1024], P(('grp', 'sub'), 'rep'), parts along dimension 1, may hold values from -6 to 6
- cache_values: bfloat16 [16, 4, 128, 1024], P(('grp', 'sub'), 'rep'), parts along dimension 1, may hold values from -6 to 6
- residual: bfloat16 [16, 4, 5120], P(('grp', 'sub'), 'rep'), parts along dimension 1, may hold values from -6 to 6
- lengths: int32 [16, 4], P(('grp', 'sub'), 'rep'), parts along dimension 1, may hold values from 3 to 128
- expert_ids: int32 [16, 4, 1], P(('grp', 'sub'), 'rep'), parts along dimension 1, may hold values from 0 to 3; in each aligned block of 2 rows (0 to 1, 2 to 3, ..., all dimensions but the last counted through in order) at most 2 rows name the same one
- capacity: int32 [4], replicated, may hold values from 1 to 2
- norm_gain: float32 [5120], replicated, may hold values from 0.5 to 1.5
- router: bfloat16 [5120, 4], replicated, may hold values from -0.078125 to 0.078125
- shared_gate: bfloat16 [5120, 8192], P(None, ('grp', 'sub')), may hold values from -0.078125 to 0.078125
- shared_up: bfloat16 [5120, 8192], P(None, ('grp', 'sub')), may hold values from -0.078125 to 0.078125
- shared_down: bfloat16 [8192, 5120], P(('grp', 'sub')), may hold values from -0.0625 to 0.0625
- expert_gate: bfloat16 [5120, 32768], P(None, ('grp', 'sub')), may hold values from -0.078125 to 0.078125
- expert_up: bfloat16 [5120, 32768], P(None, ('grp', 'sub')), may hold values from -0.078125 to 0.078125
- expert_down: bfloat16 [32768, 5120], P(('grp', 'sub')), may hold values from -0.0625 to 0.0625
Outputs:
- layer_out: bfloat16 [16, 4, 5120], P(('grp', 'sub'), 'rep'), parts along dimension 1
There are 2 independent parts, one for each index of `rep`. A program takes and returns all parts, laid end to end along the dimension named above; an argument that names none is the same for every part. Nothing has to cross between parts.
Inputs may be any that keep to these rules, and one draw needn't show every extreme that they name: `expert_ids`: in each aligned block of 2 rows (the rows of one device), no expert is named more than 2 times.
All inputs are finite; a program needn't handle non-finite values.
Results may differ from a plain program's by a relative error of at most 0.0075.
Values may be sent and summed in bfloat16 or wider, within the bound.
A program may use at most 128 MiB of HBM per device.

v0:
```python
import jax
import jax.numpy as jnp
from jax import lax
from jax.sharding import PartitionSpec as P

D = 5120
HEADS = 40
KV_HEADS = 8
HEAD = 128
EXPERTS = 4
EH = 8192


def attend(query_rows, cache_keys, cache_values, lengths):
    request_count = query_rows.shape[0]
    context = cache_keys.shape[1]
    groups = HEADS // KV_HEADS
    queries_f = query_rows.astype(jnp.float32).reshape(request_count, KV_HEADS, groups, HEAD)
    keys_f = cache_keys.astype(jnp.float32).reshape(request_count, context, KV_HEADS, HEAD)
    scores = jnp.einsum("rkgh,rjkh->rkgj", queries_f, keys_f) * HEAD ** (-0.5)
    key_pos = jnp.arange(context, dtype=jnp.int32)
    allowed = (key_pos[None, :] < lengths[:, None])[:, None, None, :]
    scores = jnp.where(allowed, scores, -1e30)
    row_peak = jnp.max(scores, axis=-1, keepdims=True)
    exponent = jnp.where(allowed, jnp.exp(scores - row_peak), 0.0)
    weights = (exponent / jnp.sum(exponent, axis=-1, keepdims=True)).astype(jnp.bfloat16)
    values_f = cache_values.astype(jnp.float32).reshape(request_count, context, KV_HEADS, HEAD)
    attended = jnp.einsum("rkgj,rjkh->rkgh", weights.astype(jnp.float32), values_f)
    return attended.reshape(request_count, HEADS * HEAD).astype(jnp.bfloat16)


def rms_normalize(stream, norm_gain):
    mean_square = jnp.mean(stream * stream, axis=-1, keepdims=True)
    return (stream * lax.rsqrt(mean_square + 1e-05) * norm_gain).astype(jnp.bfloat16)


def swiglu(inputs, w_gate, w_up, w_down):
    gate_part = jnp.dot(inputs, w_gate, preferred_element_type=jnp.float32)
    up_part = jnp.dot(inputs, w_up, preferred_element_type=jnp.float32)
    hidden = (jax.nn.silu(gate_part) * up_part).astype(jnp.bfloat16)
    return jnp.dot(hidden, w_down, preferred_element_type=jnp.float32)


def gated_inputs(flat_rows, router, route_ids):
    logits = jnp.dot(flat_rows, router, preferred_element_type=jnp.float32)
    onehot = route_ids[:, None] == jnp.arange(EXPERTS, dtype=jnp.int32)[None, :]
    picked = jnp.sum(jnp.where(onehot, logits, 0.0), axis=-1)
    return (flat_rows.astype(jnp.float32) * jax.nn.sigmoid(picked)[:, None]).astype(jnp.bfloat16)


def row_ranks(route_ids, capacity):
    onehot = (route_ids[:, None] == jnp.arange(EXPERTS, dtype=jnp.int32)[None, :]).astype(jnp.int32)
    before = jnp.cumsum(onehot, axis=0) - onehot
    row_rank = jnp.sum(before * onehot, axis=1)
    row_limit = jnp.sum(onehot * capacity[None, :], axis=1)
    return (row_rank, row_rank < row_limit)


def per_device(
    query_rows,
    cache_keys,
    cache_values,
    residual,
    lengths,
    expert_ids,
    capacity,
    norm_gain,
    router,
    shared_gate,
    shared_up,
    shared_down,
    expert_gate,
    expert_up,
    expert_down,
):
    tok_count = query_rows.shape[1]
    attended = attend(query_rows[0], cache_keys[0], cache_values[0], lengths[0])
    stream = residual[0].astype(jnp.float32) + attended.astype(jnp.float32)
    flat_rows = rms_normalize(stream, norm_gain)
    route_ids = expert_ids[0].reshape(tok_count)
    gathered, all_ids = (
        lax.all_gather(flat_rows, ("grp", "sub"), axis=0, tiled=True),
        lax.all_gather(route_ids, ("grp", "sub"), axis=0, tiled=True),
    )
    all_scaled = gated_inputs(gathered, router, all_ids)
    rank_unused, kept_all = jax.vmap(row_ranks, in_axes=(0, None))(
        all_ids.reshape(-1, tok_count), capacity
    )
    own_expert = lax.axis_index(("grp", "sub")) * expert_gate.shape[1] // EH
    usable = (all_ids == own_expert) & kept_all.reshape(-1)
    masked = jnp.where(usable[:, None], all_scaled, jnp.zeros_like(all_scaled))
    shared_part = swiglu(gathered, shared_gate, shared_up, shared_down)
    branch_sum = lax.psum_scatter(
        shared_part + swiglu(masked, expert_gate, expert_up, expert_down),
        ("grp", "sub"),
        scatter_dimension=0,
        tiled=True,
    )
    layer_out = stream + branch_sum
    return layer_out.astype(jnp.bfloat16).reshape(1, tok_count, D)


def solution(mesh):
    placed = (
        P(("grp", "sub"), "rep", None),
        P(("grp", "sub"), "rep", None, None),
        P(("grp", "sub"), "rep", None, None),
        P(("grp", "sub"), "rep", None),
        P(("grp", "sub"), "rep"),
        P(("grp", "sub"), "rep", None),
        P(),
        P(),
        P(),
        P(None, ("grp", "sub")),
        P(None, ("grp", "sub")),
        P(("grp", "sub"), None),
        P(None, ("grp", "sub")),
        P(None, ("grp", "sub")),
        P(("grp", "sub"), None),
    )
    return jax.shard_map(
        per_device,
        mesh=mesh,
        in_specs=placed,
        out_specs=P(("grp", "sub"), "rep", None),
        check_vma=False,
    )
```

profile of v0, /device:TPU:0, one launch (start us, length us, event | category | flops | bytes accessed | tf_op | source)
XLA Modules:
  0.0 184.4 jit_solution(740923644199911297)
XLA Ops:
  6.5 0.0 copy-start
  6.5 0.0 all-reduce.4.cloned.1.call-start
  6.5 1.4 fusion.38
  8.6 0.8 bitcast_dynamic-update-slice_fusion
  9.4 13.7 %all-reduce = s32[32]{0:T(128)S(1)} all-reduce(s32[32]{0:T(128)S(1)} %bitcast_dynamic-update-slice_fusion), channel_id=2, replica_groups=mesh['rep'=2,'grp'=8,'sub'=2] {'grp','sub'}, use_global_device_ids=true, to_apply=%add | all-reduce | flops 32 | bytes 256 | tf_op jit(solution)/shard_map/all_gather | solution.py:83
  23.1 0.1 eq.36
  23.2 0.1 copy.24
  23.3 0.7 select_reduce_fusion
  24.1 0.1 copy.25
  24.2 0.1 lt.31
  24.3 0.7 iota_compare_fusion.3
  25.0 1.1 copy.26
  26.1 0.8 reshape.66
  26.9 0.4 fusion.5
  27.3 0.2 fusion.39
  27.5 1.1 copy.27
  28.6 0.3 fusion.7
  29.0 0.9 multiply_reduce_fusion
  29.9 0.8 fusion.29
  30.7 18.8 %all-gather.1 = bf16[16,2,5120]{2,1,0:T(2,128)(2,1)S(1)} all-gather(bf16[1,2,5120]{2,1,0:T(2,128)(2,1)S(1)} %fusion.29), channel_id=1, replica_groups=mesh['rep'=2,'grp'=8,'sub'=2] {'grp','sub'}, dimensions={0}, use_global_device_ids=true | all-gather | bytes 348160 | tf_op jit(solution)/shard_map/all_gather | solution.py:82
  49.6 0.1 reshape.78
  49.7 0.0 copy-done
  49.7 0.2 fusion.9
  49.9 3.5 %fusion.41 = f32[32,512]{1,0:T(8,128)S(1)} fusion(bf16[32,5120]{1,0:T(8,128)(2,1)S(1)} %reshape.78, bf16[5120,512]{1,0:T(8,128)(2,1)} %param.24), kind=kOutput, calls=%fused_computation.59 | convolution fusion | flops 167772160 | bytes 5636096 | tf_op jit(solution)/shard_map/dot_general | solution.py:38
  53.4 8.9 %fusion.36 = f32[32,2048]{1,0:T(8,128)S(1)} fusion(bf16[5120,2048]{1,0:T(8,128)(2,1)} %param.27, bf16[32,5120]{1,0:T(8,128)(2,1)S(1)} %reshape.78, f32[32]{0:T(128)S(1)} %add_divide_fusion, pred[32]{0:T(512)(128)(4,1)S(1)} %compare_and_fusion), kind=kOutput, calls=%fused_computation.55 | convolution fusion | flops 671744000 | bytes 21561504 | tf_op jit(solution)/shard_map/dot_general | solution.py:38
  62.4 0.0 copy-start.2
  62.4 0.0 copy-start.1
  62.4 16.8 %fusion.10 = f32[32,5120]{1,0:T(8,128)S(1)} fusion(bf16[2048,5120]{1,0:T(8,128)(2,1)} %param.29, bf16[5120,2048]{1,0:T(8,128)(2,1)} %param.28, f32[32,2048]{1,0:T(8,128)S(1)} %fusion.36, bf16[32,5120]{1,0:T(8,128)(2,1)S(1)} %reshape.78, f32[32]{0:T(128)S(1)} %add_divide_fusion, pred[32]{0:T(512)(128)(4,1)S(1)} %compare_and_fusion), kind=kOutput, calls=%fused_computation.18 | convolution fusion | flops 1343225856 | bytes 43188384 | tf_op jit(solution)/shard_map/dot_general | solution.py:41
  79.2 6.9 %convolution_add_fusion = f32[32,5120]{1,0:T(8,128)} fusion(f32[32,5120]{1,0:T(8,128)S(1)} %fusion.10, bf16[512,5120]{1,0:T(8,128)(2,1)} %param.26, bf16[32,5120]{1,0:T(8,128)(2,1)S(1)} %reshape.78, bf16[5120,512]{1,0:T(8,128)(2,1)} %param.25, f32[32,512]{1,0:T(8,128)S(1)} %fusion.41), kind=kOutput, calls=%fused_computation.1 | convolution fusion | flops 335806464 | bytes 12189696 | tf_op jit(solution)/shard_map/dot_general | solution.py:41
  86.1 0.0 all-reduce.4.cloned.1.call-update
  86.8 89.3 %all-reduce.4.cloned.1.call-done = f32[32,5120]{1,0:T(8,128)} async-done(((f32[32,5120]{1,0:T(8,128)}), f32[32,5120]{1,0:T(8,128)}) %all-reduce.4.cloned.1.call-update) | async-done | bytes 655376
  176.0 0.0 copy-done.2
  176.0 1.6 fusion.28
  177.6 0.0 copy-done.1
  (7 shorter events, 0.1 us)
Async XLA Ops:
  6.5 43.2 %copy-start = (bf16[5120,4]{0,1:T(4,128)(2,1)S(1)}, bf16[5120,4]{0,1:T(4,128)(2,1)}, u32[]{:S(2)}) copy-start(bf16[5120,4]{0,1:T(4,128)(2,1)} %param.23) | copy-start | bytes 122884
  6.5 169.5 %all-reduce.4.cloned.1.call-start = ((), (), s32[]{:S(2)}) async-start(), calls=%async_computation | async-start | bytes 1310720
  62.4 113.6 %copy-start.2 = (bf16[1,2,5120]{2,1,0:T(2,128)(2,1)S(1)}, bf16[1,2,5120]{2,1,0:T(2,128)(2,1)}, u32[]{:S(2)}) copy-start(bf16[1,2,5120]{2,1,0:T(2,128)(2,1)} %param.18) | copy-start | bytes 61444
  62.4 115.2 %copy-start.1 = (bf16[5120,4]{0,1:T(4,128)(2,1)S(1)}, bf16[5120,4]{0,1:T(4,128)(2,1)}, u32[]{:S(2)}) copy-start(bf16[5120,4]{0,1:T(4,128)(2,1)} %param.23) | copy-start | bytes 122884
Sparse Core Ops, SparseCore 0:
  86.2 89.7 all-reduce.3
where the time goes:
time: 185 us; the launch traced here: 184 us
  waiting for transfers between devices  89.3 us (48%)
  matrix products  37 us (20%)
  blocking collectives  32.6 us (18%)
  between operations  14.8 us (8%)
  local copies, waits for them, and re-layouts  5.71 us (3%)
  other arithmetic  5.03 us (3%)
    unnamed x2, waiting for transfers between devices  89.3 us
    dot_general x2, matrix products, swiglu(): return jnp.dot(hidden, w_down, preferred_element_type=jnp.float32)  23.7 us
    all_gather x1, blocking collectives, per_device(): lax.all_gather(flat_rows, ('grp', 'sub'), axis=0, tiled=True)  18.8 us
    all_gather x1, blocking collectives, per_device(): lax.all_gather(route_ids, ('grp', 'sub'), axis=0, tiled=True)  13.7 us
    dot_general x2, matrix products, swiglu(): gate_part = jnp.dot(inputs, w_gate, preferred_element_type=jnp.float32)  12.4 us
    unnamed x12, local copies, waits for them, and re-layouts  4.56 us
  transfers between devices with their start and end apart: 1, of which 1 were waited for; matrix products, arithmetic and copies ran while one was open for 0% of the time, Pallas kernels for 0%

commit v1 on v0

--- a/solution.py
+++ b/solution.py
@@ -1,6 +1,10 @@
+import functools
+
 import jax
 import jax.numpy as jnp
 from jax import lax
+from jax.experimental import pallas as pl
+from jax.experimental.pallas import tpu as pltpu
 from jax.sharding import PartitionSpec as P
 
 D = 5120
@@ -100,6 +104,340 @@
     return layer_out.astype(jnp.bfloat16).reshape(1, tok_count, D)
 
 
+def fused_layer(sizes, *refs):
+    (q_in, k_in, v_in, res_in, len_in, ids_in, cap_in, gain_in, router_in,
+     sg_in, su_in, sd_in, eg_in, eu_in, ed_in, out_ref,
+     slots, q_raw, res_raw, router_raw, gain_v, len_s, ids_s, cap_s,
+     rows_a, rows_b, stream_v, router_f, gathered, gates, gathered_f, x_v, hidden, gate_part,
+     stage, own_part, send_buf, recv_buf,
+     small_sem, kv_sem, a_sem, b_sem, gs_sem, gr_sem, ts_sem, tr_sem, rs_sem, rr_sem) = refs
+    subs, peers, tok = sizes
+    width = slots.shape[2]
+    depth = slots.shape[1]
+    slot_count = slots.shape[0]
+    lanes = 128
+    heads = D // lanes
+    groups = HEADS // KV_HEADS
+    context = k_in.shape[2]
+    shared_w, expert_w = sg_in.shape[1], eg_in.shape[1]
+    pairs = 1 + expert_w // width
+    half = depth // 2
+    down_rows = shared_w + expert_w
+    chunk = 2 * width
+    chunks = D // chunk
+    tiles = chunk // lanes
+    total = peers * tok
+    f32, bf16 = jnp.float32, jnp.bfloat16
+
+    rep = lax.axis_index("rep")
+    me = lax.axis_index("grp") * subs + lax.axis_index("sub")
+
+    def device(p):
+        return (rep, p // subs, p % subs)
+
+    small = [
+        pltpu.make_async_copy(src, dst, small_sem.at[i])
+        for i, (src, dst) in enumerate((
+            (q_in, q_raw), (res_in, res_raw), (len_in, len_s), (ids_in, ids_s),
+            (cap_in, cap_s), (gain_in, gain_v), (router_in, router_raw)))
+    ]
+    for copy in small:
+        copy.start()
+
+    kv_slot = slot_count - 1
+    kv_cols = KV_HEADS * HEAD // width
+    kv_copies = []
+    for which, ref in enumerate((k_in, v_in)):
+        for r in range(tok):
+            for b in range(kv_cols):
+                at = ((which * tok + r) * kv_cols + b)
+                copy = pltpu.make_async_copy(
+                    ref.at[0, r, :, pl.ds(b * width, width)],
+                    slots.at[kv_slot, pl.ds(at * context, context), :],
+                    kv_sem.at[at])
+                copy.start()
+                kv_copies.append(copy)
+
+    def a_copy(s, h):
+        p, up = s // 2, s % 2
+        rows = pl.ds(h * half, half)
+        if p == 0:
+            src = (su_in if up else sg_in).at[rows, :]
+        else:
+            src = (eu_in if up else eg_in).at[rows, pl.ds((p - 1) * width, width)]
+        return pltpu.make_async_copy(src, slots.at[s, rows, :], a_sem.at[s, h])
+
+    def b_slot(j):
+        return lax.rem(2 * pairs + j, slot_count)
+
+    def b_start(j):
+        s = (2 * pairs + j) % slot_count
+        for h in range(2):
+            cols = pl.ds(j * chunk + h * width, width)
+            pltpu.make_async_copy(
+                sd_in.at[:, cols], slots.at[s, pl.ds(h * down_rows, shared_w), :],
+                b_sem.at[j, h, 0]).start()
+            pltpu.make_async_copy(
+                ed_in.at[:, cols], slots.at[s, pl.ds(h * down_rows + shared_w, expert_w), :],
+                b_sem.at[j, h, 1]).start()
+
+    for s in range(2 * pairs):
+        for h in range(2):
+            a_copy(s, h).start()
+    ahead = slot_count - 1 - 2 * pairs
+    for j in range(ahead):
+        b_start(j)
+
+    barrier = pltpu.get_barrier_semaphore()
+
+    def greet(k, carry):
+        pl.semaphore_signal(barrier, inc=1, device_id=device(lax.rem(me + k, peers)),
+                            device_id_type=pl.DeviceIdType.MESH)
+        return carry
+
+    lax.fori_loop(1, peers, greet, 0)
+
+    for copy in small:
+        copy.wait()
+    rows_a[...] = jnp.zeros_like(rows_a)
+    for c in range(heads):
+        cols = pl.ds(c * lanes, lanes)
+        rows_a[pl.ds(c, tok, stride=heads), :] = q_raw[0, :, cols].astype(f32)
+        stream_v[pl.ds(c, tok, stride=heads), :] = res_raw[0, :, cols].astype(f32)
+        router_f[pl.ds(c, EXPERTS, stride=heads), :] = router_raw[:, cols].astype(f32)
+    for copy in kv_copies:
+        copy.wait()
+
+    def cache(which, r, g):
+        b, inner = divmod(g * HEAD, width)
+        at = (which * tok + r) * kv_cols + b
+        return slots[kv_slot, at * context:(at + 1) * context, inner:inner + HEAD]
+
+    for r in range(tok):
+        for g in range(KV_HEADS):
+            at = r * heads + g * groups
+            rows_b[at:at + 8, :] = lax.dot_general(
+                rows_a[at:at + 8, :].astype(bf16), cache(0, r, g),
+                (((1,), (1,)), ((), ())), preferred_element_type=f32)
+    scores = rows_b[0:tok * heads, :] * HEAD ** (-0.5)
+    row_of = lax.broadcasted_iota(jnp.int32, scores.shape, 0)
+    limit = jnp.full(scores.shape, len_s[0, 0], jnp.int32)
+    for r in range(1, tok):
+        limit = jnp.where(row_of >= r * heads, len_s[0, r], limit)
+    allowed = lax.broadcasted_iota(jnp.int32, scores.shape, 1) < limit
+    scores = jnp.where(allowed, scores, -1e30)
+    exponent = jnp.where(allowed, jnp.exp(scores - jnp.max(scores, axis=1, keepdims=True)), 0.0)
+    rows_a[0:tok * heads, :] = exponent / jnp.sum(exponent, axis=1, keepdims=True)
+    for r in range(tok):
+        for g in range(KV_HEADS):
+            at = r * heads + g * groups
+            rows_b[at:at + 8, :] = jnp.dot(
+                rows_a[at:at + 8, :].astype(bf16), cache(1, r, g), preferred_element_type=f32)
+    for j in range(ahead, min(ahead + 1, chunks)):
+        b_start(j)
+    stream = stream_v[...] + rows_b[0:tok * heads, :].astype(bf16).astype(f32)
+    stream_v[...] = stream
+    ids = [ids_s[0, r] for r in range(tok)]
+    normed_rows = []
+    for r in range(tok):
+        part = stream[r * heads:(r + 1) * heads, :]
+        square = jnp.sum(jnp.sum(part * part, axis=0, keepdims=True), axis=1, keepdims=True) / D
+        normed_rows.append((part * lax.rsqrt(square + 1e-05) * gain_v[...]).astype(bf16))
+    gathered[me] = jnp.concatenate([n.astype(f32) for n in normed_rows], axis=0).astype(bf16)
+    gate_rows = []
+    for r in range(tok):
+        normed_f = normed_rows[r].astype(f32)
+        picked = jnp.zeros((1, 1), f32)
+        row_limit = jnp.int32(0)
+        for e in range(EXPERTS):
+            prod = normed_f * router_f[e * heads:(e + 1) * heads, :]
+            logit = jnp.sum(jnp.sum(prod, axis=0, keepdims=True), axis=1, keepdims=True)
+            match = (ids[r] == e).astype(jnp.int32)
+            picked = picked + logit * match.astype(f32)
+            row_limit = row_limit + match * cap_s[e]
+        rank = jnp.int32(0)
+        for b in range(r):
+            rank = rank + (ids[b] == ids[r]).astype(jnp.int32)
+        kept = (rank < row_limit).astype(jnp.int32)
+        sig = jnp.broadcast_to(1.0 / (1.0 + jnp.exp(-picked)), (1, lanes))
+        for e in range(EXPERTS):
+            gate_rows.append(sig * (kept * (ids[r] == e).astype(jnp.int32)).astype(f32))
+    gate_tile = jnp.concatenate(gate_rows, axis=0)
+    gates[me] = gate_tile
+
+    pl.semaphore_wait(barrier, peers - 1)
+
+    def remote(src, dst, ssem, rsem, p):
+        return pltpu.make_async_remote_copy(
+            src_ref=src, dst_ref=dst, send_sem=ssem, recv_sem=rsem,
+            device_id=device(p), device_id_type=pl.DeviceIdType.MESH)
+
+    def spread(k, carry):
+        p = lax.rem(me + k, peers)
+        remote(gathered.at[me], gathered.at[me], gs_sem.at[p], gr_sem.at[me], p).start()
+        remote(gates.at[me], gates.at[me], ts_sem.at[p], tr_sem.at[me], p).start()
+        return carry
+
+    lax.fori_loop(1, peers, spread, 0)
+    rows_per = tok * heads
+    gathered_f[pl.ds(pl.multiple_of(me * rows_per, 8), rows_per), :] = gathered[me].astype(f32)
+
+    def collect(k, carry):
+        p = lax.rem(me + peers - k, peers)
+        remote(gathered.at[p], gathered.at[p], gs_sem.at[p], gr_sem.at[p], p).wait_recv()
+        remote(gates.at[p], gates.at[p], ts_sem.at[p], tr_sem.at[p], p).wait_recv()
+        gathered_f[pl.ds(pl.multiple_of(p * rows_per, 8), rows_per), :] = gathered[p].astype(f32)
+        return carry
+
+    lax.fori_loop(1, peers, collect, 0)
+
+    own_expert = me * expert_w // EH
+    gate_all = gates[...].reshape(peers * tok * EXPERTS, lanes)
+    stage[0:peers * tok * EXPERTS, :] = gate_all
+    gate = jnp.zeros((total, lanes), f32)
+    for e in range(EXPERTS):
+        mine = (own_expert == e).astype(f32)
+        gate = gate + mine * stage[pl.ds(e, total, stride=EXPERTS), :]
+    for c in range(heads):
+        piece = gathered_f[pl.ds(c, total, stride=heads), :]
+        x_v[0, :, c * lanes:(c + 1) * lanes] = piece.astype(bf16)
+        x_v[1, :, c * lanes:(c + 1) * lanes] = (piece * gate).astype(bf16)
+
+    def a_wait(s, h):
+        view = slots.at[s, pl.ds(h * half, half), :]
+        pltpu.make_async_copy(view, view, a_sem.at[s, h]).wait()
+
+    def up_dot(s, which):
+        a_wait(s, 0)
+        first = jnp.dot(x_v[which, :, 0:half], slots[s, 0:half, :], preferred_element_type=f32)
+        a_wait(s, 1)
+        return first + jnp.dot(x_v[which, :, half:depth], slots[s, half:depth, :],
+                               preferred_element_type=f32)
+
+    def up_pair(p, carry):
+        which = jnp.minimum(p, 1)
+        gate_part[...] = up_dot(2 * p, which)
+        up = up_dot(2 * p + 1, which)
+        g = gate_part[...]
+        hidden[:, pl.ds(pl.multiple_of(p * width, width), width)] = (
+            g / (1.0 + jnp.exp(-g)) * up).astype(bf16)
+        return carry
+
+    issued = ahead + 1
+    done = 0
+    while issued < chunks:
+        up_pair(done, 0)
+        done += 1
+        for j in range(issued, min(issued + 2, chunks)):
+            b_start(j)
+        issued = min(issued + 2, chunks)
+    lax.fori_loop(done, pairs, up_pair, 0)
+
+    def down(j, carry):
+        s = b_slot(j)
+        for h in range(2):
+            view = slots.at[s, pl.ds(h * down_rows, shared_w), :]
+            pltpu.make_async_copy(view, view, b_sem.at[j, h, 0]).wait()
+            view = slots.at[s, pl.ds(h * down_rows + shared_w, expert_w), :]
+            pltpu.make_async_copy(view, view, b_sem.at[j, h, 1]).wait()
+            part = jnp.dot(hidden[...], slots[s, h * down_rows:(h + 1) * down_rows, :],
+                           preferred_element_type=f32)
+            for c in range(tiles // 2):
+                stage[pl.ds(h * (tiles // 2) + c, total, stride=tiles), :] = (
+                    part[:, c * lanes:(c + 1) * lanes])
+        rows = tok * tiles
+        own_part[j] = stage[pl.ds(pl.multiple_of(me * rows, 8), rows), :]
+        send_buf[j] = stage[...].reshape(peers, rows, lanes).astype(bf16)
+
+        def push(k, carry):
+            p = lax.rem(me + k, peers)
+            remote(send_buf.at[j, p], recv_buf.at[j, me], rs_sem.at[j, p], rr_sem.at[j, me], p).start()
+            return carry
+
+        return lax.fori_loop(1, peers, push, carry)
+
+    lax.fori_loop(0, chunks, down, 0)
+
+    for j in range(chunks):
+        def pull(k, acc):
+            p = lax.rem(me + peers - k, peers)
+            remote(send_buf.at[j, p], recv_buf.at[j, p], rs_sem.at[j, p], rr_sem.at[j, p], p).wait_recv()
+            return acc + recv_buf[j, p].astype(f32)
+
+        acc = lax.fori_loop(1, peers, pull, own_part[j])
+        for r in range(tok):
+            rows = slice(r * heads + j * tiles, r * heads + (j + 1) * tiles)
+            rows_b[rows, :] = stream_v[rows, :] + acc[r * tiles:(r + 1) * tiles, :]
+    out_ref[...] = rows_b[0:tok * heads, :].astype(bf16)
+
+    def drain(k, carry):
+        p = lax.rem(me + k, peers)
+        remote(gathered.at[me], gathered.at[me], gs_sem.at[p], gr_sem.at[me], p).wait_send()
+        remote(gates.at[me], gates.at[me], ts_sem.at[p], tr_sem.at[me], p).wait_send()
+        for j in range(chunks):
+            remote(send_buf.at[j, p], recv_buf.at[j, me], rs_sem.at[j, p], rr_sem.at[j, me], p).wait_send()
+        return carry
+
+    lax.fori_loop(1, peers, drain, 0)
+
+
+def fused_fits(mesh, tok, shared_w, expert_w):
+    peers = mesh.shape["grp"] * mesh.shape["sub"]
+    chunk = 2 * shared_w
+    return (peers > 1 and shared_w % 256 == 0 and expert_w % shared_w == 0
+            and 2 * (shared_w + expert_w) <= D and D % chunk == 0
+            and (KV_HEADS * HEAD) % shared_w == 0 and tok * (chunk // 128) % 16 == 0
+            and (chunk // 128) % 8 == 0
+            and (tok * EXPERTS) % 8 == 0 and tok * HEADS % 16 == 0 and EH % expert_w == 0
+            and peers * tok <= 64)
+
+
+def fused_call(mesh, *args):
+    (query_rows, cache_keys, cache_values, residual, lengths, expert_ids, capacity, norm_gain,
+     router, sg, su, sd, eg, eu, ed) = args
+    tok = query_rows.shape[1]
+    subs = mesh.shape["sub"]
+    peers = mesh.shape["grp"] * subs
+    width, expert_w = sg.shape[1], eg.shape[1]
+    pairs = 1 + expert_w // width
+    chunk = 2 * width
+    chunks = D // chunk
+    rows = tok * (chunk // 128)
+    heads = D // 128
+    total = peers * tok
+    slot_count = 2 * pairs + 1
+    f32, bf16 = jnp.float32, jnp.bfloat16
+    V, DMA = pltpu.VMEM, pltpu.SemaphoreType.DMA
+    kv = 2 * tok * (KV_HEADS * HEAD // width)
+    out = pl.pallas_call(
+        functools.partial(fused_layer, (subs, peers, tok)),
+        out_shape=jax.ShapeDtypeStruct((tok * heads, 128), bf16),
+        in_specs=[pl.BlockSpec(memory_space=pl.ANY)] * 15,
+        out_specs=pl.BlockSpec(memory_space=pltpu.VMEM),
+        scratch_shapes=[
+            V((slot_count, D, width), bf16),
+            V((1, tok, D), bf16), V((1, tok, D), bf16), V((EXPERTS, D), bf16), V((heads, 128), f32),
+            pltpu.SMEM((1, tok), jnp.int32), pltpu.SMEM((1, tok), jnp.int32),
+            pltpu.SMEM((EXPERTS,), jnp.int32),
+            V((tok * heads + 8, 128), f32), V((tok * heads + 8, 128), f32), V((tok * heads, 128), f32),
+            V((EXPERTS * heads, 128), f32),
+            V((peers, tok * heads, 128), bf16), V((peers, tok * EXPERTS, 128), f32),
+            V((peers * tok * heads, 128), f32), V((2, total, D), bf16),
+            V((total, width + expert_w), bf16), V((total, width), f32),
+            V((peers * rows, 128), f32), V((chunks, rows, 128), f32),
+            V((chunks, peers, rows, 128), bf16), V((chunks, peers, rows, 128), bf16),
+            DMA((7,)), DMA((kv,)), DMA((2 * pairs, 2)), DMA((chunks, 2, 2)),
+            DMA((peers,)), DMA((peers,)), DMA((peers,)), DMA((peers,)),
+            DMA((chunks, peers)), DMA((chunks, peers)),
+        ],
+        compiler_params=pltpu.CompilerParams(
+            collective_id=0, has_side_effects=True, vmem_limit_bytes=67043328),
+        name="fused_layer",
+    )(query_rows, cache_keys, cache_values, residual, lengths, expert_ids.reshape(1, tok), capacity,
+      norm_gain.reshape(heads, 128), router.T, sg, su, sd, eg, eu, ed)
+    return out.reshape(1, tok, D)
+
+
 def solution(mesh):
     placed = (
         P(("grp", "sub"), "rep", None),
@@ -118,8 +456,14 @@
         P(None, ("grp", "sub")),
         P(("grp", "sub"), None),
     )
+
+    def body(*args):
+        if fused_fits(mesh, args[0].shape[1], args[9].shape[1], args[12].shape[1]):
+            return fused_call(mesh, *args)
+        return per_device(*args)
+
     return jax.shard_map(
-        per_device,
+        body,
         mesh=mesh,
         in_specs=placed,
         out_specs=P(("grp", "sub"), "rep", None),

time: 185 us -> 57.4 us (0.31)
  waiting for transfers between devices: 89.3 us -> 0 us
  Pallas kernels: 0 us -> 55.9 us
  matrix products: 37 us -> 0 us
  blocking collectives: 32.6 us -> 0 us
  between operations: 14.8 us -> 0.01 us
  other arithmetic: 5.03 us -> 0 us
  local copies, waits for them, and re-layouts: 5.71 us -> 1.35 us
    unnamed x2 -> x0, waiting for transfers between devices: 89.3 us -> none
    pallas_call x0 -> x1, Pallas kernels: none -> 55.9 us  [fused_call(): pl.pallas_call(functools.partial(fused_layer, (subs, peers, tok)), out_sh...]
    dot_general x7 -> x0, matrix products: 37 us -> none  [the longest x2 23.7 us: swiglu(): return jnp.dot(hidden, w_down, preferred_element_type=jnp.float32)]
    all_gather x2 -> x0, blocking collectives: 32.6 us -> none  [the longest x1 18.8 us: per_device(): lax.all_gather(flat_rows, ('grp', 'sub'), axis=0, tiled=True)]
    unnamed x12 -> x0, local copies, waits for them, and re-layouts: 4.56 us -> none
  transfers between devices with their start and end apart: 1 -> 0, of which waited for: 1 -> 0; matrix products, arithmetic and copies ran while one was open for 0% -> 0% of each run, Pallas kernels for 0% -> 0%
where the time goes in v1:
time: 57.4 us; the launch traced here: 57.2 us
  Pallas kernels  55.9 us (97%)
  local copies, waits for them, and re-layouts  1.35 us (2%)
    pallas_call x1, Pallas kernels, fused_call(): pl.pallas_call(functools.partial(fused_layer, (subs, peers, tok)), out_sh...  55.9 us
    reshape x1, local copies, waits for them, and re-layouts, fused_call(): return out.reshape(1, tok, D)  1.35 us

profile of v1, /device:TPU:0, one launch (start us, length us, event | category | flops | bytes accessed | tf_op | source)
XLA Modules:
  0.0 57.2 jit_solution(8126574037339284343)
XLA Ops:
  0.0 55.9 %fused_layer.1 = bf16[80,128]{1,0:T(8,128)(2,1)} custom-call(bf16[1,2,5120]{2,1,0:T(2,128)(2,1)} %refs_0_.1, bf16[1,2,128,1024]{3,2,1,0:T(8,128)(2,1)} %refs_1_.1, bf16[1,2,128,1024]{3,2,1,0:T(8,128)(2,1)} %refs_2_.1, bf16[1,2,5120]{2,1,0:T(2,128)(2,1)} %refs_3_.1, s32[1,2]{1,0:T(1,128)} %refs_4_.1, s32[1,2]{1,0:T(1,128)} %bitcast.5, s32[4]{0:T(128)} %refs_6_.1, ...), custom_call_target="tpu_custom_call" | custom-call | tf_op jit(solution)/shard_map/fused_layer/pallas_call | solution.py:412
  55.9 1.3 %reshape.11 = bf16[1,2,5120]{2,1,0:T(2,128)(2,1)} reshape(bf16[80,128]{1,0:T(8,128)(2,1)} %fused_layer.1) | data formatting | bytes 40960 | tf_op jit(solution)/shard_map/reshape | solution.py:438

commit v2 on v1

--- a/solution.py
+++ b/solution.py
@@ -110,7 +110,8 @@
      slots, q_raw, res_raw, router_raw, gain_v, len_s, ids_s, cap_s,
      rows_a, rows_b, stream_v, router_f, gathered, gates, gathered_f, x_v, hidden, gate_part,
      stage, own_part, send_buf, recv_buf,
-     small_sem, kv_sem, a_sem, b_sem, gs_sem, gr_sem, ts_sem, tr_sem, rs_sem, rr_sem) = refs
+     small_sem, kv_sem, a_sem, b_sem, gs_sem, gr_sem, ts_sem, tr_sem, fs_sem, ft_sem,
+     rs_sem, rr_sem) = refs
     subs, peers, tok = sizes
     width = slots.shape[2]
     depth = slots.shape[1]
@@ -127,6 +128,7 @@
     chunks = D // chunk
     tiles = chunk // lanes
     total = peers * tok
+    lag = min(2, chunks)
     f32, bf16 = jnp.float32, jnp.bfloat16
 
     rep = lax.axis_index("rep")
@@ -176,14 +178,14 @@
             cols = pl.ds(j * chunk + h * width, width)
             pltpu.make_async_copy(
                 sd_in.at[:, cols], slots.at[s, pl.ds(h * down_rows, shared_w), :],
-                b_sem.at[j, h, 0]).start()
+                b_sem.at[j, h, 0]).start(priority=1)
             pltpu.make_async_copy(
                 ed_in.at[:, cols], slots.at[s, pl.ds(h * down_rows + shared_w, expert_w), :],
-                b_sem.at[j, h, 1]).start()
+                b_sem.at[j, h, 1]).start(priority=1)
 
     for s in range(2 * pairs):
         for h in range(2):
-            a_copy(s, h).start()
+            a_copy(s, h).start(priority=1)
     ahead = slot_count - 1 - 2 * pairs
     for j in range(ahead):
         b_start(j)
@@ -272,24 +274,60 @@
             src_ref=src, dst_ref=dst, send_sem=ssem, recv_sem=rsem,
             device_id=device(p), device_id_type=pl.DeviceIdType.MESH)
 
+    chips = peers // subs
+    chip, sub = me // subs, lax.rem(me, subs)
+    partners = [chip * subs + lax.rem(sub + o, subs) for o in range(1, subs)]
+
+    def share(block, p, rows_sem, gate_sem):
+        return (remote(gathered.at[block], gathered.at[block], rows_sem, gr_sem.at[block], p),
+                remote(gates.at[block], gates.at[block], gate_sem, tr_sem.at[block], p))
+
+    def own_share(p):
+        return share(me, p, gs_sem.at[p], ts_sem.at[p])
+
+    def ahead_chip(k):
+        return lax.rem(chip + k, chips) * subs + sub
+
     def spread(k, carry):
-        p = lax.rem(me + k, peers)
-        remote(gathered.at[me], gathered.at[me], gs_sem.at[p], gr_sem.at[me], p).start()
-        remote(gates.at[me], gates.at[me], ts_sem.at[p], tr_sem.at[me], p).start()
-        return carry
-
-    lax.fori_loop(1, peers, spread, 0)
+        for copy in own_share(ahead_chip(k)):
+            copy.start()
+        return carry
+
+    lax.fori_loop(1, chips, spread, 0)
+    for p in partners:
+        for copy in own_share(p):
+            copy.start()
     rows_per = tok * heads
-    gathered_f[pl.ds(pl.multiple_of(me * rows_per, 8), rows_per), :] = gathered[me].astype(f32)
+
+    def unpack(p):
+        gathered_f[pl.ds(pl.multiple_of(p * rows_per, 8), rows_per), :] = gathered[p].astype(f32)
+
+    unpack(me)
+
+    def forward(block, o):
+        return share(block, partners[o], fs_sem.at[block, o], ft_sem.at[block, o])
 
     def collect(k, carry):
-        p = lax.rem(me + peers - k, peers)
-        remote(gathered.at[p], gathered.at[p], gs_sem.at[p], gr_sem.at[p], p).wait_recv()
-        remote(gates.at[p], gates.at[p], ts_sem.at[p], tr_sem.at[p], p).wait_recv()
-        gathered_f[pl.ds(pl.multiple_of(p * rows_per, 8), rows_per), :] = gathered[p].astype(f32)
-        return carry
-
-    lax.fori_loop(1, peers, collect, 0)
+        p = ahead_chip(chips - k)
+        for copy in share(p, p, gs_sem.at[p], ts_sem.at[p]):
+            copy.wait_recv()
+        for o in range(subs - 1):
+            for copy in forward(p, o):
+                copy.start()
+        unpack(p)
+        return carry
+
+    lax.fori_loop(1, chips, collect, 0)
+
+    def collect_near(k, carry):
+        for o in range(1, subs):
+            p = lax.rem(chip + chips - k, chips) * subs + lax.rem(sub + o, subs)
+            for copy in share(p, p, gs_sem.at[p], ts_sem.at[p]):
+                copy.wait_recv()
+            unpack(p)
+        return carry
+
+    lax.fori_loop(0, chips, collect_near, 0)
 
     own_expert = me * expert_w // EH
     gate_all = gates[...].reshape(peers * tok * EXPERTS, lanes)
@@ -332,6 +370,33 @@
             b_start(j)
         issued = min(issued + 2, chunks)
     lax.fori_loop(done, pairs, up_pair, 0)
+
+    def sent(k, carry):
+        p = ahead_chip(k)
+        for copy in own_share(p):
+            copy.wait_send()
+        for o in range(subs - 1):
+            for copy in forward(p, o):
+                copy.wait_send()
+        return carry
+
+    lax.fori_loop(1, chips, sent, 0)
+    for p in partners:
+        for copy in own_share(p):
+            copy.wait_send()
+
+    def finish(j):
+        def pull(k, acc):
+            p = lax.rem(me + peers - k, peers)
+            copy = remote(send_buf.at[j, p], recv_buf.at[j, p], rs_sem.at[j, p], rr_sem.at[j, p], p)
+            copy.wait_send()
+            copy.wait_recv()
+            return acc + recv_buf[j, p].astype(f32)
+
+        acc = lax.fori_loop(1, peers, pull, own_part[j], unroll=True)
+        for r in range(tok):
+            rows = pl.ds(pl.multiple_of(r * heads + j * tiles, 8), tiles)
+            rows_b[rows, :] = stream_v[rows, :] + acc[r * tiles:(r + 1) * tiles, :]
 
     def down(j, carry):
         s = b_slot(j)
@@ -354,31 +419,19 @@
             remote(send_buf.at[j, p], recv_buf.at[j, me], rs_sem.at[j, p], rr_sem.at[j, me], p).start()
             return carry
 
-        return lax.fori_loop(1, peers, push, carry)
+        lax.fori_loop(1, peers, push, 0, unroll=True)
+
+        @pl.when(j >= lag)
+        def _():
+            finish(j - lag)
+
+        return carry
 
     lax.fori_loop(0, chunks, down, 0)
 
-    for j in range(chunks):
-        def pull(k, acc):
-            p = lax.rem(me + peers - k, peers)
-            remote(send_buf.at[j, p], recv_buf.at[j, p], rs_sem.at[j, p], rr_sem.at[j, p], p).wait_recv()
-            return acc + recv_buf[j, p].astype(f32)
-
-        acc = lax.fori_loop(1, peers, pull, own_part[j])
-        for r in range(tok):
-            rows = slice(r * heads + j * tiles, r * heads + (j + 1) * tiles)
-            rows_b[rows, :] = stream_v[rows, :] + acc[r * tiles:(r + 1) * tiles, :]
+    for j in range(chunks - lag, chunks):
+        finish(j)
     out_ref[...] = rows_b[0:tok * heads, :].astype(bf16)
-
-    def drain(k, carry):
-        p = lax.rem(me + k, peers)
-        remote(gathered.at[me], gathered.at[me], gs_sem.at[p], gr_sem.at[me], p).wait_send()
-        remote(gates.at[me], gates.at[me], ts_sem.at[p], tr_sem.at[me], p).wait_send()
-        for j in range(chunks):
-            remote(send_buf.at[j, p], recv_buf.at[j, me], rs_sem.at[j, p], rr_sem.at[j, me], p).wait_send()
-        return carry
-
-    lax.fori_loop(1, peers, drain, 0)
 
 
 def fused_fits(mesh, tok, shared_w, expert_w):
@@ -428,6 +481,7 @@
             V((chunks, peers, rows, 128), bf16), V((chunks, peers, rows, 128), bf16),
             DMA((7,)), DMA((kv,)), DMA((2 * pairs, 2)), DMA((chunks, 2, 2)),
             DMA((peers,)), DMA((peers,)), DMA((peers,)), DMA((peers,)),
+            DMA((peers, max(subs - 1, 1))), DMA((peers, max(subs - 1, 1))),
             DMA((chunks, peers)), DMA((chunks, peers)),
         ],
         compiler_params=pltpu.CompilerParams(

time: 57.4 us -> 41.9 us (0.73)
  Pallas kernels: 55.9 us -> 40.4 us
    pallas_call x1, Pallas kernels: 55.9 us -> 40.4 us  [fused_call(): pl.pallas_call(functools.partial(fused_layer, (subs, peers, tok)), out_sh...]
where the time goes in v2:
time: 41.9 us; the launch traced here: 41.8 us
  Pallas kernels  40.4 us (96%)
  local copies, waits for them, and re-layouts  1.35 us (3%)
    pallas_call x1, Pallas kernels, fused_call(): pl.pallas_call(functools.partial(fused_layer, (subs, peers, tok)), out_sh...  40.4 us
    reshape x1, local copies, waits for them, and re-layouts, fused_call(): return out.reshape(1, tok, D)  1.35 us

profile of v2, /device:TPU:0, one launch (start us, length us, event | category | flops | bytes accessed | tf_op | source)
XLA Modules:
  0.0 41.8 jit_solution(4373207378790829671)
XLA Ops:
  0.0 40.4 %fused_layer.1 = bf16[80,128]{1,0:T(8,128)(2,1)} custom-call(bf16[1,2,5120]{2,1,0:T(2,128)(2,1)} %refs_0_.1, bf16[1,2,128,1024]{3,2,1,0:T(8,128)(2,1)} %refs_1_.1, bf16[1,2,128,1024]{3,2,1,0:T(8,128)(2,1)} %refs_2_.1, bf16[1,2,5120]{2,1,0:T(2,128)(2,1)} %refs_3_.1, s32[1,2]{1,0:T(1,128)} %refs_4_.1, s32[1,2]{1,0:T(1,128)} %bitcast.5, s32[4]{0:T(128)} %refs_6_.1, ...), custom_call_target="tpu_custom_call" | custom-call | tf_op jit(solution)/shard_map/fused_layer/pallas_call | solution.py:465
  40.4 1.3 %reshape.11 = bf16[1,2,5120]{2,1,0:T(2,128)(2,1)} reshape(bf16[80,128]{1,0:T(8,128)(2,1)} %fused_layer.1) | data formatting | bytes 40960 | tf_op jit(solution)/shard_map/reshape | solution.py:492

commit v3 on v2

--- a/solution.py
+++ b/solution.py
@@ -128,7 +128,7 @@
     chunks = D // chunk
     tiles = chunk // lanes
     total = peers * tok
-    lag = min(2, chunks)
+    lag = min(4, chunks)
     f32, bf16 = jnp.float32, jnp.bfloat16
 
     rep = lax.axis_index("rep")

time: 41.9 us -> 40.8 us (0.974)
  Pallas kernels: 40.4 us -> 39.3 us
    pallas_call x1, Pallas kernels: 40.4 us -> 39.3 us  [fused_call(): pl.pallas_call(functools.partial(fused_layer, (subs, peers, tok)), out_sh...]
where the time goes in v3:
time: 40.8 us; the launch traced here: 40.6 us
  Pallas kernels  39.3 us (96%)
  local copies, waits for them, and re-layouts  1.35 us (3%)
    pallas_call x1, Pallas kernels, fused_call(): pl.pallas_call(functools.partial(fused_layer, (subs, peers, tok)), out_sh...  39.3 us
    reshape x1, local copies, waits for them, and re-layouts, fused_call(): return out.reshape(1, tok, D)  1.35 us

profile of v3, /device:TPU:0, one launch (start us, length us, event | category | flops | bytes accessed | tf_op | source)
XLA Modules:
  0.0 40.6 jit_solution(5646421121525393304)
XLA Ops:
  0.0 39.3 %fused_layer.1 = bf16[80,128]{1,0:T(8,128)(2,1)} custom-call(bf16[1,2,5120]{2,1,0:T(2,128)(2,1)} %refs_0_.1, bf16[1,2,128,1024]{3,2,1,0:T(8,128)(2,1)} %refs_1_.1, bf16[1,2,128,1024]{3,2,1,0:T(8,128)(2,1)} %refs_2_.1, bf16[1,2,5120]{2,1,0:T(2,128)(2,1)} %refs_3_.1, s32[1,2]{1,0:T(1,128)} %refs_4_.1, s32[1,2]{1,0:T(1,128)} %bitcast.5, s32[4]{0:T(128)} %refs_6_.1, ...), custom_call_target="tpu_custom_call" | custom-call | tf_op jit(solution)/shard_map/fused_layer/pallas_call | solution.py:465
  39.3 1.3 %reshape.11 = bf16[1,2,5120]{2,1,0:T(2,128)(2,1)} reshape(bf16[80,128]{1,0:T(8,128)(2,1)} %fused_layer.1) | data formatting | bytes 40960 | tf_op jit(solution)/shard_map/reshape | solution.py:492
